TPU v7x, 32 devices: a whole 2x2x4 slice. The times are simulated.
32 devices in a mesh: member: 8 (over z, core), dp: 4 (over y, x).
Axes of the slice: x: 2, y: 2, z: 4, core: 2. Of those that a mesh axis runs over, the one named last changes fastest.
Arguments:
- feats: bfloat16 [8, 2048, 1024], P('member', 'dp'), may hold values from -160 to 160
- pair_weight: float32 [8, 3], replicated, may hold values from 0.5 to 2
Outputs:
- grad_centred: float32 [8, 2048, 1024], P('member', 'dp')
- cka: float32 [8, 3], P('member')
All inputs are finite; a program needn't handle non-finite values.
Results may differ from a plain program's by a relative error of at most 0.0053.
Values may be sent and summed in bfloat16 or wider, within the bound.
A program may use at most 128 MiB of HBM per device.

v0:
```python
import math
import jax
import jax.numpy as jnp
from jax import lax
from jax.sharding import PartitionSpec as P


def mixing(self_hsic, pair_hsic, pair_weight):
    pairs = pair_weight.shape[1]
    members = pair_weight.shape[0]
    partner_self = jnp.stack([jnp.roll(self_hsic, -o) for o in range(1, pairs + 1)], axis=1)
    norms = jnp.sqrt(self_hsic[:, None] * partner_self)
    cka = pair_hsic / norms
    weighted = pair_weight * cka
    incoming = sum((jnp.roll(weighted[:, o - 1], o) for o in range(1, pairs + 1)))
    self_coef = (jnp.sum(weighted, axis=1) + incoming) / (self_hsic + 1e-06)
    coef = 2.0 * pair_weight / norms
    eye = jnp.eye(members, dtype=jnp.float32)
    mix = -2.0 * self_coef[:, None] * eye
    for o in range(1, pairs + 1):
        ahead = coef[:, o - 1][:, None] * jnp.roll(eye, o, axis=1)
        mix = mix + ahead + ahead.T
    return (cka, mix)


def shards(feats, pair_weight):
    rows = feats[0]
    members = lax.axis_size("member")
    pairs = pair_weight.shape[1]
    whole = lax.all_gather(rows, "dp", axis=0, tiled=True)
    batch, width = whole.shape
    mean = jnp.sum(whole.astype(jnp.float32), axis=0) / batch
    centred = (whole.astype(jnp.float32) - mean).astype(jnp.bfloat16)
    own = (rows.astype(jnp.float32) - mean).astype(jnp.bfloat16)
    blocks = centred.reshape(members, batch // members, width)
    gram = jnp.einsum("rf,mcf->mrc", own, blocks, preferred_element_type=jnp.float32)
    held = lax.all_to_all(gram.astype(jnp.bfloat16), "member", 0, 0)
    held = held.astype(jnp.float32)
    sums = []
    for o in range(pairs + 1):
        sums.append(jnp.sum(held * jnp.roll(held, -o, axis=0), axis=(1, 2)))
    sums = lax.psum(jnp.stack(sums, axis=1), ("member", "dp"))
    cka, mix = mixing(sums[:, 0], sums[:, 1:], pair_weight)
    mixed = jnp.stack(
        [sum((mix[m, q] * held[q] for q in range(members))) for m in range(members)]
    ).astype(jnp.bfloat16)
    mixed = lax.all_to_all(mixed, "member", 0, 0)
    grad = jnp.einsum("jrc,jcf->rf", mixed, blocks, preferred_element_type=jnp.float32)
    grad = math.sqrt(batch) * grad
    own_cka = lax.dynamic_slice_in_dim(cka, lax.axis_index("member"), 1, axis=0)
    return (grad[None], own_cka)


def solution(mesh):
    return jax.shard_map(
        shards,
        mesh=mesh,
        in_specs=(P("member", "dp", None), P()),
        out_specs=(P("member", "dp", None), P("member", None)),
        check_vma=False,
    )
```

profile of v0, /device:TPU:0, one launch (start us, length us, event | category | flops | bytes accessed | tf_op | source)
XLA Modules:
  0.0 292.4 jit_solution(5384150362921916437)
XLA Ops:
  7.9 57.2 %all-gather.3.cloned.1.call-done = bf16[1,2048,1024]{2,1,0:T(8,128)(2,1)} async-done(((bf16[1,512,1024]{2,1,0:T(8,128)(2,1)}), bf16[1,2048,1024]{2,1,0:T(8,128)(2,1)}) %all-gather.3.cloned.1.call-update) | async-done | bytes 4194320 | tf_op jit(solution)/shard_map/all_gather | solution.py:30
  65.1 3.0 %convert_reduce_fusion = f32[1024]{0:T(1024)S(1)} fusion(bf16[1,2048,1024]{2,1,0:T(8,128)(2,1)} %all-gather.3.cloned.1.call-done), kind=kLoop, calls=%fused_computation | loop fusion | flops 4193280 | bytes 4198400 | tf_op jit(solution)/shard_map/reduce_sum | solution.py:32
  68.6 1.3 fusion.1
  69.9 1.9 copy-done
  71.8 3.8 %convert_bitcast_fusion.1 = bf16[8,512,256]{1,2,0:T(8,128)(2,1)} fusion(bf16[8,256,1024]{2,1,0:T(8,128)(2,1)S(1)} %bitcast.136, bf16[1,512,1024]{2,1,0:T(8,128)(2,1)S(1)} %copy-done.2, f32[1024]{0:T(1024)S(1)} %broadcast_multiply_fusion), kind=kOutput, calls=%fused_computation.13 | convolution fusion | flops 2150105088 | bytes 7344128 | tf_op jit(solution)/shard_map/rf,mcf->mrc/dot_general | solution.py:36
  75.5 4.6 %all-to-all-start = ((bf16[8,512,256]{1,2,0:T(8,128)(2,1)}), bf16[8,512,256]{1,2,0:T(8,128)(2,1)S(1)}, u32[]{:S(2)}, u32[]{:S(2)}) async-start(bf16[8,512,256]{1,2,0:T(8,128)(2,1)} %convert_bitcast_fusion.1), calls=%async_computation | async-start | bytes 4194304 | tf_op jit(solution)/shard_map/all_to_all | solution.py:37
  80.5 48.6 %all-to-all-done = bf16[8,512,256]{1,2,0:T(8,128)(2,1)S(1)} async-done(((bf16[8,512,256]{1,2,0:T(8,128)(2,1)}), bf16[8,512,256]{1,2,0:T(8,128)(2,1)S(1)}, u32[]{:S(2)}, u32[]{:S(2)}) %all-to-all-start) | async-done | bytes 2097184 | tf_op jit(solution)/shard_map/all_to_all | solution.py:37
  130.9 1.8 multiply_reduce_fusion
  132.8 37.0 %psum.7 = f32[8,4]{0,1:T(4,128)S(1)} all-reduce(f32[8,4]{0,1:T(4,128)S(1)} %pad_maximum_fusion), channel_id=1, replica_groups=mesh['member'=8,'dp'=4] {'member','dp'}, use_global_device_ids=true, to_apply=%region_5.6 | all-reduce | flops 32 | bytes 256 | tf_op jit(solution)/shard_map/psum | solution.py:42
  170.5 0.7 maximum_bitcast_fusion
  172.2 0.7 slice_bitcast_fusion.1
  173.3 0.7 fusion.26
  175.4 0.7 fusion.24
  176.7 6.4 %fusion.9 = bf16[8,512,256]{1,2,0:T(8,128)(2,1)} fusion(f32[8,512,256]{1,2,0:T(8,128)S(1)} %convert_element_type.47, f32[]{:T(128)} %bitcast.34, f32[]{:T(128)} %bitcast.33, f32[]{:T(128)} %bitcast.32, f32[]{:T(128)} %bitcast.31, f32[]{:T(128)} %bitcast.30, f32[]{:T(128)} %bitcast.29, f32[]{:T(128)} %bitcast.28, f32[]{:T(128)} %bitcast.27), kind=kLoop, calls=%fused_computation.25 | loop fusion | flops 2097151 | bytes 4456480
  183.1 6.1 %fusion.10 = bf16[8,512,256]{1,2,0:T(8,128)(2,1)} fusion(bf16[8,512,256]{1,2,0:T(8,128)(2,1)} %fusion.9, f32[8,512,256]{1,2,0:T(8,128)S(1)} %convert_element_type.47, f32[]{:T(128)} %bitcast.42, f32[]{:T(128)} %bitcast.41, f32[]{:T(128)} %bitcast.40, f32[]{:T(128)} %bitcast.39, f32[]{:T(128)} %bitcast.38, f32[]{:T(128)} %bitcast.37, f32[]{:T(128)} %bitcast.36, ...), kind=kLoop, calls=%fused_computation.26 | loop fusion | flops 2097152 | bytes 4460544
  189.2 6.1 %fusion.11 = bf16[8,512,256]{1,2,0:T(8,128)(2,1)} fusion(bf16[8,512,256]{1,2,0:T(8,128)(2,1)} %fusion.10, f32[8,512,256]{1,2,0:T(8,128)S(1)} %convert_element_type.47, f32[]{:T(128)} %bitcast.50, f32[]{:T(128)} %bitcast.49, f32[]{:T(128)} %bitcast.48, f32[]{:T(128)} %bitcast.47, f32[]{:T(128)} %bitcast.46, f32[]{:T(128)} %bitcast.45, f32[]{:T(128)} %bitcast.44, ...), kind=kLoop, calls=%fused_computation.27 | loop fusion | flops 2097152 | bytes 4460544
  195.3 6.1 %fusion.12 = bf16[8,512,256]{1,2,0:T(8,128)(2,1)} fusion(bf16[8,512,256]{1,2,0:T(8,128)(2,1)} %fusion.11, f32[8,512,256]{1,2,0:T(8,128)S(1)} %convert_element_type.47, f32[]{:T(128)} %bitcast.58, f32[]{:T(128)} %bitcast.57, f32[]{:T(128)} %bitcast.56, f32[]{:T(128)} %bitcast.55, f32[]{:T(128)} %bitcast.54, f32[]{:T(128)} %bitcast.53, f32[]{:T(128)} %bitcast.52, ...), kind=kLoop, calls=%fused_computation.28 | loop fusion | flops 2097152 | bytes 4460544
  201.4 6.3 %fusion.13 = bf16[8,512,256]{1,2,0:T(8,128)(2,1)} fusion(bf16[8,512,256]{1,2,0:T(8,128)(2,1)} %fusion.12, f32[8,512,256]{1,2,0:T(8,128)S(1)} %convert_element_type.47, f32[]{:T(128)} %bitcast.66, f32[]{:T(128)} %bitcast.65, f32[]{:T(128)} %bitcast.64, f32[]{:T(128)} %bitcast.63, f32[]{:T(128)} %bitcast.62, f32[]{:T(128)} %bitcast.61, f32[]{:T(128)} %bitcast.60, ...), kind=kLoop, calls=%fused_computation.29 | loop fusion | flops 2097152 | bytes 4460544
  207.7 6.2 %fusion.14 = bf16[8,512,256]{1,2,0:T(8,128)(2,1)} fusion(bf16[8,512,256]{1,2,0:T(8,128)(2,1)} %fusion.13, f32[8,512,256]{1,2,0:T(8,128)S(1)} %convert_element_type.47, f32[]{:T(128)} %bitcast.74, f32[]{:T(128)} %bitcast.73, f32[]{:T(128)} %bitcast.72, f32[]{:T(128)} %bitcast.71, f32[]{:T(128)} %bitcast.70, f32[]{:T(128)} %bitcast.69, f32[]{:T(128)} %bitcast.68, ...), kind=kLoop, calls=%fused_computation.30 | loop fusion | flops 2097152 | bytes 4460544
  214.0 6.2 %fusion.15 = bf16[8,512,256]{1,2,0:T(8,128)(2,1)} fusion(bf16[8,512,256]{1,2,0:T(8,128)(2,1)} %fusion.14, f32[8,512,256]{1,2,0:T(8,128)S(1)} %convert_element_type.47, f32[]{:T(128)} %bitcast.82, f32[]{:T(128)} %bitcast.81, f32[]{:T(128)} %bitcast.80, f32[]{:T(128)} %bitcast.79, f32[]{:T(128)} %bitcast.78, f32[]{:T(128)} %bitcast.77, f32[]{:T(128)} %bitcast.76, ...), kind=kLoop, calls=%fused_computation.31 | loop fusion | flops 2097152 | bytes 4460544
  220.2 6.2 %fusion.16 = bf16[8,512,256]{1,2,0:T(8,128)(2,1)} fusion(bf16[8,512,256]{1,2,0:T(8,128)(2,1)} %fusion.15, f32[8,512,256]{1,2,0:T(8,128)S(1)} %convert_element_type.47, f32[]{:T(128)} %bitcast.90, f32[]{:T(128)} %bitcast.89, f32[]{:T(128)} %bitcast.88, f32[]{:T(128)} %bitcast.87, f32[]{:T(128)} %bitcast.86, f32[]{:T(128)} %bitcast.85, f32[]{:T(128)} %bitcast.84, ...), kind=kLoop, calls=%fused_computation.32 | loop fusion | flops 2097152 | bytes 4460544 | tf_op jit(solution)/shard_map/stack | solution.py:44
  226.4 4.2 %all-to-all-start.1 = ((bf16[8,512,256]{1,2,0:T(8,128)(2,1)}), bf16[8,512,256]{1,2,0:T(8,128)(2,1)S(1)}, u32[]{:S(2)}, u32[]{:S(2)}) async-start(bf16[8,512,256]{1,2,0:T(8,128)(2,1)} %fusion.16), calls=%async_computation.1 | async-start | bytes 4194304 | tf_op jit(solution)/shard_map/all_to_all | solution.py:47
  231.3 48.4 %all-to-all-done.1 = bf16[8,512,256]{1,2,0:T(8,128)(2,1)S(1)} async-done(((bf16[8,512,256]{1,2,0:T(8,128)(2,1)}), bf16[8,512,256]{1,2,0:T(8,128)(2,1)S(1)}, u32[]{:S(2)}, u32[]{:S(2)}) %all-to-all-start.1) | async-done | bytes 2097184 | tf_op jit(solution)/shard_map/all_to_all | solution.py:47
  279.7 5.9 %fusion.5 = f32[1,512,1024]{2,1,0:T(8,128)} fusion(bf16[8,512,256]{1,2,0:T(8,128)(2,1)S(1)} %all-to-all-done.1, bf16[8,256,1024]{2,1,0:T(8,128)(2,1)} %bitcast.137), kind=kOutput, calls=%fused_computation.12 | convolution fusion | flops 2148007936 | bytes 8388608 | tf_op jit(solution)/shard_map/jrc,jcf->rf/dot_general | solution.py:48
  (53 shorter events, 8.0 us)
Async XLA Ops:
  7.2 58.0 %all-gather.3.cloned.1.call-start = ((), (), s32[]{:S(2)}) async-start(), calls=%async_computation.2 | async-start | bytes 5242880 | tf_op jit(solution)/shard_map/all_gather | solution.py:30
  65.1 3.4 %copy-start.1 = (bf16[1,2048,1024]{2,1,0:T(8,128)(2,1)S(1)}, bf16[1,2048,1024]{2,1,0:T(8,128)(2,1)}, u32[]{:S(2)}) copy-start(bf16[1,2048,1024]{2,1,0:T(8,128)(2,1)} %all-gather.3.cloned.1.call-done) | copy-start | bytes 12582916
  68.6 3.2 %copy-start.2 = (bf16[1,512,1024]{2,1,0:T(8,128)(2,1)S(1)}, bf16[1,512,1024]{2,1,0:T(8,128)(2,1)}, u32[]{:S(2)}) copy-start(bf16[1,512,1024]{2,1,0:T(8,128)(2,1)} %param.2) | copy-start | bytes 3145732
  69.9 1.9 copy-start
  75.5 53.6 %all-to-all-start = ((bf16[8,512,256]{1,2,0:T(8,128)(2,1)}), bf16[8,512,256]{1,2,0:T(8,128)(2,1)S(1)}, u32[]{:S(2)}, u32[]{:S(2)}) async-start(bf16[8,512,256]{1,2,0:T(8,128)(2,1)} %convert_bitcast_fusion.1), calls=%async_computation | async-start | bytes 4194304 | tf_op jit(solution)/shard_map/all_to_all | solution.py:37
  130.9 40.5 %copy-start.3 = (f32[8,3]{0,1:T(4,128)S(1)}, f32[8,3]{0,1:T(4,128)}, u32[]{:S(2)}) copy-start(f32[8,3]{0,1:T(4,128)} %param.3) | copy-start | bytes 292
  226.4 53.3 %all-to-all-start.1 = ((bf16[8,512,256]{1,2,0:T(8,128)(2,1)}), bf16[8,512,256]{1,2,0:T(8,128)(2,1)S(1)}, u32[]{:S(2)}, u32[]{:S(2)}) async-start(bf16[8,512,256]{1,2,0:T(8,128)(2,1)} %fusion.16), calls=%async_computation.1 | async-start | bytes 4194304 | tf_op jit(solution)/shard_map/all_to_all | solution.py:47
Sparse Core Ops, SparseCore 0:
  9.8 55.2 all-gather.2
where the time goes:
time: 293 us; the launch traced here: 292 us
  waiting for transfers between devices  155 us (53%)
  other arithmetic  58.2 us (20%)
  blocking collectives  37 us (13%)
  between operations  14.1 us (5%)
  local copies, waits for them, and re-layouts  9.6 us (3%)
  matrix products  9.6 us (3%)
  starting transfers between devices  8.86 us (3%)
    all_gather x1, waiting for transfers between devices, shards(): whole = lax.all_gather(rows, 'dp', axis=0, tiled=True)  57.2 us
    all_to_all x1, waiting for transfers between devices, shards(): held = lax.all_to_all(gram.astype(jnp.bfloat16), 'member', 0, 0)  48.6 us
    all_to_all x1, waiting for transfers between devices, shards(): mixed = lax.all_to_all(mixed, 'member', 0, 0)  48.4 us
    unnamed x7, other arithmetic  43.5 us
    psum x1, blocking collectives, shards(): sums = lax.psum(jnp.stack(sums, axis=1), ('member', 'dp'))  37 us
    another operation x1, other arithmetic, shards(): jnp.stack([sum((mix[m, q] * held[q] for q in range(members))) for m in ra...  6.23 us
  transfers between devices with their start and end apart: 3, of which 3 were waited for; matrix products, arithmetic and copies ran while one was open for 0% of the time, Pallas kernels for 0%

commit v1 on v0

--- a/solution.py
+++ b/solution.py
@@ -27,7 +27,13 @@
     rows = feats[0]
     members = lax.axis_size("member")
     pairs = pair_weight.shape[1]
-    whole = lax.all_gather(rows, "dp", axis=0, tiled=True)
+    devices = lax.axis_size("dp")
+    block, pieces = (rows, [rows])
+    for _ in range(devices - 1):
+        block = lax.ppermute(block, "dp", [(i, (i + 1) % devices) for i in range(devices)])
+        pieces.insert(0, block)
+    line = jnp.concatenate(pieces, axis=0)
+    whole = jnp.roll(line, (lax.axis_index("dp") + 1) * rows.shape[0], axis=0)
     batch, width = whole.shape
     mean = jnp.sum(whole.astype(jnp.float32), axis=0) / batch
     centred = (whole.astype(jnp.float32) - mean).astype(jnp.bfloat16)

time: 293 us -> 299 us (1.020)
  waiting for transfers between devices: 155 us -> 170 us
  between operations: 14.1 us -> 0.82 us
  starting transfers between devices: 8.86 us -> 12.5 us
    ppermute x0 -> x3, waiting for transfers between devices: none -> 73.2 us  [shards(): lax.ppermute(block, 'dp', [(i, (i + 1) % devices) for i in range(devices)])]
    all_gather x1 -> x0, waiting for transfers between devices: 57.2 us -> none  [shards(): whole = lax.all_gather(rows, 'dp', axis=0, tiled=True)]
    ppermute x0 -> x3, starting transfers between devices: none -> 3.8 us  [shards(): lax.ppermute(block, 'dp', [(i, (i + 1) % devices) for i in range(devices)])]
  transfers between devices with their start and end apart: 3 -> 5, of which waited for: 3 -> 5; matrix products, arithmetic and copies ran while one was open for 0% -> 0% of each run, Pallas kernels for 0% -> 0%
where the time goes in v1:
time: 299 us; the launch traced here: 298 us
  waiting for transfers between devices  170 us (57%)
  other arithmetic  56 us (19%)
  blocking collectives  37 us (12%)
  starting transfers between devices  12.5 us (4%)
  local copies, waits for them, and re-layouts  12.2 us (4%)
  matrix products  9.6 us (3%)
    ppermute x3, waiting for transfers between devices, shards(): lax.ppermute(block, 'dp', [(i, (i + 1) % devices) for i in range(devices)])  73.2 us
    all_to_all x1, waiting for transfers between devices, shards(): held = lax.all_to_all(gram.astype(jnp.bfloat16), 'member', 0, 0)  48.6 us
    all_to_all x1, waiting for transfers between devices, shards(): mixed = lax.all_to_all(mixed, 'member', 0, 0)  48.4 us
    unnamed x7, other arithmetic  43.5 us
    psum x1, blocking collectives, shards(): sums = lax.psum(jnp.stack(sums, axis=1), ('member', 'dp'))  37 us
    another operation x1, other arithmetic, shards(): jnp.stack([sum((mix[m, q] * held[q] for q in range(members))) for m in ra...  6.23 us
  transfers between devices with their start and end apart: 5, of which 5 were waited for; matrix products, arithmetic and copies ran while one was open for 0% of the time, Pallas kernels for 0%

profile of v1, /device:TPU:0, one launch (start us, length us, event | category | flops | bytes accessed | tf_op | source)
XLA Modules:
  0.0 298.3 jit_solution(5001556447284529945)
XLA Ops:
  0.6 3.0 %collective-permute-start = (bf16[512,1024]{1,0:T(8,128)(2,1)}, bf16[512,1024]{1,0:T(8,128)(2,1)S(1)}, u32[]{:S(2)}, u32[]{:S(2)}) collective-permute-start(bf16[512,1024]{1,0:T(8,128)(2,1)} %bitcast.135), channel_id=1, source_target_pairs={{0,1},{1,2},{2,3},{3,0},{4,5},{5,6},{6,7},{7,4},{8,9},{9,10},{10,1... | collective-permute-start | bytes 3145736 | tf_op jit(solution)/shard_map/ppermute | solution.py:33
  3.7 24.3 %collective-permute-done = bf16[512,1024]{1,0:T(8,128)(2,1)S(1)} collective-permute-done((bf16[512,1024]{1,0:T(8,128)(2,1)}, bf16[512,1024]{1,0:T(8,128)(2,1)S(1)}, u32[]{:S(2)}, u32[]{:S(2)}) %collective-permute-start) | collective-permute-done | bytes 1048608 | tf_op jit(solution)/shard_map/ppermute | solution.py:33
  28.8 24.4 %collective-permute-done.1 = bf16[512,1024]{1,0:T(8,128)(2,1)S(1)} collective-permute-done((bf16[512,1024]{1,0:T(8,128)(2,1)S(1)}, bf16[512,1024]{1,0:T(8,128)(2,1)S(1)}, u32[]{:S(2)}, u32[]{:S(2)}) %collective-permute-start.1) | collective-permute-done | bytes 1048608 | tf_op jit(solution)/shard_map/ppermute | solution.py:33
  53.2 24.5 %collective-permute-done.2 = bf16[512,1024]{1,0:T(8,128)(2,1)} collective-permute-done((bf16[512,1024]{1,0:T(8,128)(2,1)S(1)}, bf16[512,1024]{1,0:T(8,128)(2,1)}, u32[]{:S(2)}, u32[]{:S(2)}) %collective-permute-start.2) | collective-permute-done | bytes 1048608 | tf_op jit(solution)/shard_map/ppermute | solution.py:33
  77.7 1.3 constant_dynamic-update-slice_fusion.7
  79.2 1.3 constant_dynamic-update-slice_fusion.3
  81.5 1.3 fusion
  82.8 1.9 copy-done
  84.7 3.7 %convert_bitcast_fusion = bf16[8,512,256]{1,2,0:T(8,128)(2,1)} fusion(bf16[8,256,1024]{2,1,0:T(8,128)(2,1)S(1)} %bitcast.133, bf16[1,512,1024]{2,1,0:T(8,128)(2,1)S(1)} %copy-done.1, f32[1024]{0:T(1024)S(1)} %broadcast_multiply_fusion), kind=kOutput, calls=%fused_computation.12 | convolution fusion | flops 2150105088 | bytes 7344128 | tf_op jit(solution)/shard_map/rf,mcf->mrc/dot_general | solution.py:42
  88.5 4.5 %all-to-all-start = ((bf16[8,512,256]{1,2,0:T(8,128)(2,1)}), bf16[8,512,256]{1,2,0:T(8,128)(2,1)S(1)}, u32[]{:S(2)}, u32[]{:S(2)}) async-start(bf16[8,512,256]{1,2,0:T(8,128)(2,1)} %convert_bitcast_fusion), calls=%async_computation | async-start | bytes 4194304 | tf_op jit(solution)/shard_map/all_to_all | solution.py:43
  93.4 48.6 %all-to-all-done = bf16[8,512,256]{1,2,0:T(8,128)(2,1)S(1)} async-done(((bf16[8,512,256]{1,2,0:T(8,128)(2,1)}), bf16[8,512,256]{1,2,0:T(8,128)(2,1)S(1)}, u32[]{:S(2)}, u32[]{:S(2)}) %all-to-all-start) | async-done | bytes 2097184 | tf_op jit(solution)/shard_map/all_to_all | solution.py:43
  143.7 1.8 multiply_reduce_fusion
  145.6 37.0 %psum.7 = f32[8,4]{0,1:T(4,128)S(1)} all-reduce(f32[8,4]{0,1:T(4,128)S(1)} %pad_maximum_fusion), channel_id=1, replica_groups=mesh['member'=8,'dp'=4] {'member','dp'}, use_global_device_ids=true, to_apply=%region_5.6 | all-reduce | flops 32 | bytes 256 | tf_op jit(solution)/shard_map/psum | solution.py:48
  189.5 6.4 %fusion.8 = bf16[8,512,256]{1,2,0:T(8,128)(2,1)} fusion(f32[8,512,256]{1,2,0:T(8,128)S(1)} %convert_element_type.47, f32[]{:T(128)} %bitcast.34, f32[]{:T(128)} %bitcast.33, f32[]{:T(128)} %bitcast.32, f32[]{:T(128)} %bitcast.31, f32[]{:T(128)} %bitcast.30, f32[]{:T(128)} %bitcast.29, f32[]{:T(128)} %bitcast.28, f32[]{:T(128)} %bitcast.27), kind=kLoop, calls=%fused_computation.24 | loop fusion | flops 2097151 | bytes 4456480
  195.9 6.1 %fusion.9 = bf16[8,512,256]{1,2,0:T(8,128)(2,1)} fusion(bf16[8,512,256]{1,2,0:T(8,128)(2,1)} %fusion.8, f32[8,512,256]{1,2,0:T(8,128)S(1)} %convert_element_type.47, f32[]{:T(128)} %bitcast.42, f32[]{:T(128)} %bitcast.41, f32[]{:T(128)} %bitcast.40, f32[]{:T(128)} %bitcast.39, f32[]{:T(128)} %bitcast.38, f32[]{:T(128)} %bitcast.37, f32[]{:T(128)} %bitcast.36, ...), kind=kLoop, calls=%fused_computation.25 | loop fusion | flops 2097152 | bytes 4460544
  202.0 6.1 %fusion.10 = bf16[8,512,256]{1,2,0:T(8,128)(2,1)} fusion(bf16[8,512,256]{1,2,0:T(8,128)(2,1)} %fusion.9, f32[8,512,256]{1,2,0:T(8,128)S(1)} %convert_element_type.47, f32[]{:T(128)} %bitcast.50, f32[]{:T(128)} %bitcast.49, f32[]{:T(128)} %bitcast.48, f32[]{:T(128)} %bitcast.47, f32[]{:T(128)} %bitcast.46, f32[]{:T(128)} %bitcast.45, f32[]{:T(128)} %bitcast.44, ...), kind=kLoop, calls=%fused_computation.26 | loop fusion | flops 2097152 | bytes 4460544
  208.2 6.1 %fusion.11 = bf16[8,512,256]{1,2,0:T(8,128)(2,1)} fusion(bf16[8,512,256]{1,2,0:T(8,128)(2,1)} %fusion.10, f32[8,512,256]{1,2,0:T(8,128)S(1)} %convert_element_type.47, f32[]{:T(128)} %bitcast.58, f32[]{:T(128)} %bitcast.57, f32[]{:T(128)} %bitcast.56, f32[]{:T(128)} %bitcast.55, f32[]{:T(128)} %bitcast.54, f32[]{:T(128)} %bitcast.53, f32[]{:T(128)} %bitcast.52, ...), kind=kLoop, calls=%fused_computation.27 | loop fusion | flops 2097152 | bytes 4460544
  214.2 6.3 %fusion.12 = bf16[8,512,256]{1,2,0:T(8,128)(2,1)} fusion(bf16[8,512,256]{1,2,0:T(8,128)(2,1)} %fusion.11, f32[8,512,256]{1,2,0:T(8,128)S(1)} %convert_element_type.47, f32[]{:T(128)} %bitcast.66, f32[]{:T(128)} %bitcast.65, f32[]{:T(128)} %bitcast.64, f32[]{:T(128)} %bitcast.63, f32[]{:T(128)} %bitcast.62, f32[]{:T(128)} %bitcast.61, f32[]{:T(128)} %bitcast.60, ...), kind=kLoop, calls=%fused_computation.28 | loop fusion | flops 2097152 | bytes 4460544
  220.6 6.2 %fusion.13 = bf16[8,512,256]{1,2,0:T(8,128)(2,1)} fusion(bf16[8,512,256]{1,2,0:T(8,128)(2,1)} %fusion.12, f32[8,512,256]{1,2,0:T(8,128)S(1)} %convert_element_type.47, f32[]{:T(128)} %bitcast.74, f32[]{:T(128)} %bitcast.73, f32[]{:T(128)} %bitcast.72, f32[]{:T(128)} %bitcast.71, f32[]{:T(128)} %bitcast.70, f32[]{:T(128)} %bitcast.69, f32[]{:T(128)} %bitcast.68, ...), kind=kLoop, calls=%fused_computation.29 | loop fusion | flops 2097152 | bytes 4460544
  226.8 6.2 %fusion.14 = bf16[8,512,256]{1,2,0:T(8,128)(2,1)} fusion(bf16[8,512,256]{1,2,0:T(8,128)(2,1)} %fusion.13, f32[8,512,256]{1,2,0:T(8,128)S(1)} %convert_element_type.47, f32[]{:T(128)} %bitcast.82, f32[]{:T(128)} %bitcast.81, f32[]{:T(128)} %bitcast.80, f32[]{:T(128)} %bitcast.79, f32[]{:T(128)} %bitcast.78, f32[]{:T(128)} %bitcast.77, f32[]{:T(128)} %bitcast.76, ...), kind=kLoop, calls=%fused_computation.30 | loop fusion | flops 2097152 | bytes 4460544
  233.0 6.2 %fusion.15 = bf16[8,512,256]{1,2,0:T(8,128)(2,1)} fusion(bf16[8,512,256]{1,2,0:T(8,128)(2,1)} %fusion.14, f32[8,512,256]{1,2,0:T(8,128)S(1)} %convert_element_type.47, f32[]{:T(128)} %bitcast.90, f32[]{:T(128)} %bitcast.89, f32[]{:T(128)} %bitcast.88, f32[]{:T(128)} %bitcast.87, f32[]{:T(128)} %bitcast.86, f32[]{:T(128)} %bitcast.85, f32[]{:T(128)} %bitcast.84, ...), kind=kLoop, calls=%fused_computation.31 | loop fusion | flops 2097152 | bytes 4460544 | tf_op jit(solution)/shard_map/stack | solution.py:50
  239.2 4.2 %all-to-all-start.1 = ((bf16[8,512,256]{1,2,0:T(8,128)(2,1)}), bf16[8,512,256]{1,2,0:T(8,128)(2,1)S(1)}, u32[]{:S(2)}, u32[]{:S(2)}) async-start(bf16[8,512,256]{1,2,0:T(8,128)(2,1)} %fusion.15), calls=%async_computation.1 | async-start | bytes 4194304 | tf_op jit(solution)/shard_map/all_to_all | solution.py:53
  244.1 48.4 %all-to-all-done.1 = bf16[8,512,256]{1,2,0:T(8,128)(2,1)S(1)} async-done(((bf16[8,512,256]{1,2,0:T(8,128)(2,1)}), bf16[8,512,256]{1,2,0:T(8,128)(2,1)S(1)}, u32[]{:S(2)}, u32[]{:S(2)}) %all-to-all-start.1) | async-done | bytes 2097184 | tf_op jit(solution)/shard_map/all_to_all | solution.py:53
  292.5 5.9 %fusion.4 = f32[1,512,1024]{2,1,0:T(8,128)} fusion(bf16[8,512,256]{1,2,0:T(8,128)(2,1)S(1)} %all-to-all-done.1, bf16[8,256,1024]{2,1,0:T(8,128)(2,1)} %bitcast.134), kind=kOutput, calls=%fused_computation.11 | convolution fusion | flops 2148007936 | bytes 8388608 | tf_op jit(solution)/shard_map/jrc,jcf->rf/dot_general | solution.py:54
  (62 shorter events, 11.7 us)
Async XLA Ops:
  0.6 78.5 %copy-start.1 = (bf16[1,512,1024]{2,1,0:T(8,128)(2,1)S(1)}, bf16[1,512,1024]{2,1,0:T(8,128)(2,1)}, u32[]{:S(2)}) copy-start(bf16[1,512,1024]{2,1,0:T(8,128)(2,1)} %param.2) | copy-start | bytes 3145732
  0.6 27.4 %collective-permute-start = (bf16[512,1024]{1,0:T(8,128)(2,1)}, bf16[512,1024]{1,0:T(8,128)(2,1)S(1)}, u32[]{:S(2)}, u32[]{:S(2)}) collective-permute-start(bf16[512,1024]{1,0:T(8,128)(2,1)} %bitcast.135), channel_id=1, source_target_pairs={{0,1},{1,2},{2,3},{3,0},{4,5},{5,6},{6,7},{7,4},{8,9},{9,10},{10,1... | collective-permute-start | bytes 3145736 | tf_op jit(solution)/shard_map/ppermute | solution.py:33
  28.0 25.2 %collective-permute-start.1 = (bf16[512,1024]{1,0:T(8,128)(2,1)S(1)}, bf16[512,1024]{1,0:T(8,128)(2,1)S(1)}, u32[]{:S(2)}, u32[]{:S(2)}) collective-permute-start(bf16[512,1024]{1,0:T(8,128)(2,1)S(1)} %collective-permute-done), channel_id=1, source_target_pairs={{0,1},{1,2},{2,3},{3,0},{4,5},{5,6},{6,7},{7,4},{8,9},{9,10},{10,1... | collective-permute-start | bytes 3145736 | tf_op jit(solution)/shard_map/ppermute | solution.py:33
  53.2 24.5 %collective-permute-start.2 = (bf16[512,1024]{1,0:T(8,128)(2,1)S(1)}, bf16[512,1024]{1,0:T(8,128)(2,1)}, u32[]{:S(2)}, u32[]{:S(2)}) collective-permute-start(bf16[512,1024]{1,0:T(8,128)(2,1)S(1)} %collective-permute-done.1), channel_id=1, source_target_pairs={{0,1},{1,2},{2,3},{3,0},{4,5},{5,6},{6,7},{7,4},{8,9},{9,10},{10,1... | collective-permute-start | bytes 3145736 | tf_op jit(solution)/shard_map/ppermute | solution.py:33
  82.8 1.9 copy-start
  88.5 53.5 %all-to-all-start = ((bf16[8,512,256]{1,2,0:T(8,128)(2,1)}), bf16[8,512,256]{1,2,0:T(8,128)(2,1)S(1)}, u32[]{:S(2)}, u32[]{:S(2)}) async-start(bf16[8,512,256]{1,2,0:T(8,128)(2,1)} %convert_bitcast_fusion), calls=%async_computation | async-start | bytes 4194304 | tf_op jit(solution)/shard_map/all_to_all | solution.py:43
  143.7 40.5 %copy-start.2 = (f32[8,3]{0,1:T(4,128)S(1)}, f32[8,3]{0,1:T(4,128)}, u32[]{:S(2)}) copy-start(f32[8,3]{0,1:T(4,128)} %param.3) | copy-start | bytes 292
  239.2 53.3 %all-to-all-start.1 = ((bf16[8,512,256]{1,2,0:T(8,128)(2,1)}), bf16[8,512,256]{1,2,0:T(8,128)(2,1)S(1)}, u32[]{:S(2)}, u32[]{:S(2)}) async-start(bf16[8,512,256]{1,2,0:T(8,128)(2,1)} %fusion.15), calls=%async_computation.1 | async-start | bytes 4194304 | tf_op jit(solution)/shard_map/all_to_all | solution.py:53
